TPU v7x, 256 devices: a whole 4x4x8 slice. The times are simulated.
256 devices in a mesh: own: 32 (over y, x, core), row: 8 (over z).
Axes of the slice: x: 4, y: 4, z: 8, core: 2. Of those that a mesh axis runs over, the one named last changes fastest.
Arguments:
- weights: float32 [32, 8, 128, 2048], P('own', None, 'row'), may hold values from -200 to 200
- first_moment: float32 [32, 8, 128, 2048], P('own', None, 'row'), may hold values from -20 to 20
- second_moment: float32 [32, 8, 128, 2048], P('own', None, 'row'), may hold values from 0.002 to 0.05
- gradient: bfloat16 [32, 8, 128, 2048], P('own', None, 'row'), may hold values from -0.59765625 to 0.59765625
- owner: int32 [127], replicated, may hold values from 0 to 31, as said below
Outputs:
- new_weights: float32 [32, 8, 128, 2048], P('own', None, 'row')
- new_first: float32 [32, 8, 128, 2048], P('own', None, 'row')
- new_second: float32 [32, 8, 128, 2048], P('own', None, 'row')
- low_weights: bfloat16 [32, 8, 128, 2048], P('own')
- weight_norms: float32 [14], replicated
- update_norms: float32 [14], replicated
- trust_ratios: float32 [14], replicated
Inputs may be any that keep to these rules, and one draw needn't show every extreme that they name: No owner group holds more than 8 tiles, and one holds exactly 8.
All inputs are finite; a program needn't handle non-finite values.
Results may differ from a plain program's by a relative error of at most 0.0004.
Values may be sent and summed in bfloat16 or wider, within the bound.
A program may use at most 128 MiB of HBM per device.

v0:
```python
import jax
import jax.numpy as jnp
import numpy as np
from jax import lax
from jax.sharding import PartitionSpec as P

QW = 4096
KVW = 512
NEXP = 128
FF = 768
EW = 3
TILE = 128
MATS = 14
DECAY = 0.1
STEP_SIZE = 0.05
EPSILON = 1e-06


def matrix_table():
    counts = [QW // TILE, KVW // TILE, KVW // TILE, QW // TILE, NEXP // TILE] + [FF // TILE] * (
        3 * EW
    )
    return np.repeat(np.arange(len(counts)), counts).astype(np.int32)


def slot_select(owner, owners_count, slot_count, matrices):
    tile_table = jnp.asarray(matrix_table())
    owner_hit = (owner[:, None] == jnp.arange(owners_count, dtype=jnp.int32)[None, :]).astype(
        jnp.int32
    )
    tile_rank = jnp.sum((jnp.cumsum(owner_hit, 0) - owner_hit) * owner_hit, 1)
    slot_hit = tile_rank[:, None] == jnp.arange(slot_count, dtype=jnp.int32)[None, :]
    matrix_hit = tile_table[:, None] == jnp.arange(matrices, dtype=jnp.int32)[None, :]
    owner_bool = owner_hit > 0
    joined = (
        owner_bool[:, :, None, None] & slot_hit[:, None, :, None] & matrix_hit[:, None, None, :]
    )
    return jnp.any(joined, axis=0).astype(jnp.float32)


def shards(weights, first_moment, second_moment, gradient, owner):
    slot_count = weights.shape[1]
    select_all = slot_select(owner, lax.axis_size("own"), slot_count, MATS)
    select = lax.dynamic_index_in_dim(select_all, lax.axis_index("own"), 0, keepdims=False)
    used = jnp.sum(select, 1)[None, :, None, None]
    grad_wide = gradient.astype(jnp.float32)
    moment_one = 0.5 * first_moment + 0.5 * grad_wide
    moment_two = 0.5 * second_moment + 0.5 * grad_wide * grad_wide
    direction = moment_one / (jnp.sqrt(moment_two) + EPSILON) + DECAY * weights
    weight_sq = jnp.sum(weights * weights, axis=(2, 3))[0]
    update_sq = jnp.sum(direction * direction, axis=(2, 3))[0]
    weight_part = jnp.sum(select * weight_sq[:, None], 0)
    update_part = jnp.sum(select * update_sq[:, None], 0)
    weight_total, update_total = lax.psum((weight_part, update_part), ("own", "row"))
    weight_norms = jnp.sqrt(weight_total)
    update_norms = jnp.sqrt(update_total)
    trust_ratios = weight_norms / (update_norms + EPSILON)
    slot_ratio = jnp.sum(select * trust_ratios[None, :], 1)[None, :, None, None]
    new_weights = used * (weights - STEP_SIZE * slot_ratio * direction)
    low_weights = lax.all_gather(new_weights.astype(jnp.bfloat16), "row", axis=2, tiled=True)
    new_first = used * moment_one
    new_second = used * moment_two
    return (
        new_weights,
        new_first,
        new_second,
        low_weights,
        weight_norms,
        update_norms,
        trust_ratios,
    )


def solution(mesh):
    placed = (
        P("own", None, "row", None),
        P("own", None, "row", None),
        P("own", None, "row", None),
        P("own", None, "row", None),
        P(),
    )
    return jax.shard_map(
        shards,
        mesh=mesh,
        in_specs=placed,
        out_specs=(
            P("own", None, "row", None),
            P("own", None, "row", None),
            P("own", None, "row", None),
            P("own", None, None, None),
            P(),
            P(),
            P(),
        ),
        check_vma=False,
    )
```

profile of v0, /device:TPU:1, one launch (start us, length us, event | category | flops | bytes accessed | tf_op | source)
XLA Modules:
  0.0 167.5 jit_solution(3595493397532116743)
XLA Ops:
  7.2 0.0 copy-start
  7.2 0.0 all-gather.2.cloned.1.call-start
  7.2 0.7 iota_compare_fusion.1
  8.0 0.7 fusion.4
  8.7 0.1 copy.13
  8.8 0.2 reduce_window_sum.11
  9.0 0.8 select_reduce_fusion
  9.9 7.7 %and_reduce_fusion = pred[32,8,14]{1,2,0:T(8,128)(4,1)S(1)} fusion(pred[127,14]{0,1:T(8,128)(4,1)S(1)} %iota_compare_fusion.1, pred[127,32,8]{0,2,1:T(8,128)(4,1)S(1)} %broadcast_and_fusion), kind=kLoop, calls=%fused_computation | loop fusion | flops 906752 | bytes 37874 | tf_op jit(solution)/shard_map/reduce_or | solution.py:38
  17.7 0.1 copy.14
  17.7 4.3 %multiply_reduce_fusion = (f32[8]{0:T(128)S(1)}, f32[1,8,16,2048]{3,2,1,0:T(8,128)S(1)}, f32[1,8,16,2048]{3,2,1,0:T(8,128)}, f32[1,8,16,2048]{3,2,1,0:T(8,128)}, f32[8]{0:T(128)S(1)}) fusion(f32[1,8,16,2048]{3,2,1,0:T(8,128)} %param.6, f32[1,8,16,2048]{3,2,1,0:T(8,128)} %param.8, bf16[1,8,16,2048]{3,2,1,0:T(8,128)(2,1)} %param.9, ...), kind=kLoop, calls=%fused_computation.5 | loop fusion | flops 4456432 | bytes 6815840 | tf_op jit(solution)/shard_map/reduce_sum | solution.py:51
  22.1 0.1 fusion.6
  22.2 81.4 %all-reduce = (f32[14]{0:T(128)S(1)}, f32[14]{0:T(128)S(1)}) all-reduce(f32[14]{0:T(128)S(1)} %get-tuple-element.8, f32[14]{0:T(128)S(1)} %get-tuple-element.7), channel_id=1, replica_groups=mesh['own'=32,'row'=8] {'own','row'}, use_global_device_ids=true, to_apply=%region_6.7 | all-reduce | flops 28 | bytes 224 | tf_op jit(solution)/shard_map/psum | solution.py:54
  103.6 0.5 add_divide_fusion
  104.1 0.0 copy-start.1
  104.1 0.1 fusion.7
  104.2 0.0 copy-done
  104.2 1.4 fusion.9
  105.6 0.0 all-gather.2.cloned.1.call-update
  105.7 50.2 %all-gather.2.cloned.1.call-done = bf16[1,8,128,2048]{3,2,1,0:T(8,128)(2,1)} async-done(((bf16[1,8,16,2048]{3,2,1,0:T(8,128)(2,1)}), bf16[1,8,128,2048]{3,2,1,0:T(8,128)(2,1)}) %all-gather.2.cloned.1.call-update) | async-done | bytes 4194320 | tf_op jit(solution)/shard_map/all_gather | solution.py:60
  155.8 4.8 %copy.16 = bf16[1,8,128,2048]{3,2,1,0:T(8,128)(2,1)} copy(bf16[1,8,128,2048]{3,2,1,0:T(8,128)(2,1)} %all-gather.2.cloned.1.call-done) | data formatting | bytes 8388608
  160.6 0.0 copy-done.1
  (5 shorter events, 0.1 us)
Async XLA Ops:
  7.2 97.0 %copy-start = (f32[1,8,16,2048]{3,2,1,0:T(8,128)S(1)}, f32[1,8,16,2048]{3,2,1,0:T(8,128)}, u32[]{:S(2)}) copy-start(f32[1,8,16,2048]{3,2,1,0:T(8,128)} %param.6) | copy-start | bytes 3145732
  7.2 148.6 %all-gather.2.cloned.1.call-start = ((), (), s32[]{:S(2)}) async-start(), calls=%async_computation | async-start | bytes 4718592 | tf_op jit(solution)/shard_map/all_gather | solution.py:60
  104.1 56.5 %copy-start.1 = (f32[14]{0:T(128)}, f32[14]{0:T(128)S(1)}, u32[]{:S(2)}) copy-start(f32[14]{0:T(128)S(1)} %get-tuple-element.36) | copy-start | bytes 172
Sparse Core Ops, SparseCore 0:
  105.8 50.0 all-gather.1
where the time goes:
time: 168 us; the launch traced here: 167 us
  blocking collectives  81.4 us (48%)
  waiting for transfers between devices  50.2 us (30%)
  other arithmetic  16.8 us (10%)
  between operations  14.1 us (8%)
  local copies, waits for them, and re-layouts  4.96 us (3%)
    psum x1, blocking collectives, shards(): lax.psum((weight_part, update_part), ('own', 'row'))  81.4 us
    all_gather x1, waiting for transfers between devices, shards(): lax.all_gather(new_weights.astype(jnp.bfloat16), 'row', axis=2, tiled=True)  50.2 us
    reduce_or x1, other arithmetic, slot_select(): return jnp.any(joined, axis=0).astype(jnp.float32)  7.73 us
    unnamed x5, local copies, waits for them, and re-layouts  4.8 us
    reduce_sum x1, other arithmetic, shards(): update_sq = jnp.sum(direction * direction, axis=(2, 3))[0]  4.33 us
  transfers between devices with their start and end apart: 1, of which 1 were waited for; matrix products, arithmetic and copies ran while one was open for 0% of the time, Pallas kernels for 0%

commit v1 on v0

--- a/solution.py
+++ b/solution.py
@@ -14,6 +14,9 @@
 DECAY = 0.1
 STEP_SIZE = 0.05
 EPSILON = 1e-06
+note_the_figure = lambda local_block: jnp.concatenate(
+    lax.all_to_all(jnp.stack([local_block for _ in range(lax.axis_size("row"))]), "row", 0, 0), 2
+)
 
 
 def matrix_table():
@@ -57,7 +60,7 @@
     trust_ratios = weight_norms / (update_norms + EPSILON)
     slot_ratio = jnp.sum(select * trust_ratios[None, :], 1)[None, :, None, None]
     new_weights = used * (weights - STEP_SIZE * slot_ratio * direction)
-    low_weights = lax.all_gather(new_weights.astype(jnp.bfloat16), "row", axis=2, tiled=True)
+    low_weights = note_the_figure(new_weights.astype(jnp.bfloat16))
     new_first = used * moment_one
     new_second = used * moment_two
     return (

time: 168 us -> 200 us (1.19)
  blocking collectives: 81.4 us -> 180 us
  waiting for transfers between devices: 50.2 us -> 0 us
  between operations: 14.1 us -> 0.71 us
    all_to_all x0 -> x1, blocking collectives: none -> 98.3 us  [lax.all_to_all(jnp.stack([local_block for _ in range(lax.axis_size('row')...]
    all_gather x1 -> x0, waiting for transfers between devices: 50.2 us -> none  [shards(): lax.all_gather(new_weights.astype(jnp.bfloat16), 'row', axis=2, tiled=True)]
    unnamed x5 -> x4, local copies, waits for them, and re-layouts: 4.8 us -> 0.01 us
    all_to_all x0 -> x1, local copies, waits for them, and re-layouts: none -> 2.32 us  [lax.all_to_all(jnp.stack([local_block for _ in range(lax.axis_size('row')...]
  transfers between devices with their start and end apart: 1 -> 0, of which waited for: 1 -> 0; matrix products, arithmetic and copies ran while one was open for 0% -> 0% of each run, Pallas kernels for 0% -> 0%
where the time goes in v1:
time: 200 us
  blocking collectives  180 us (90%)
  other arithmetic  16.6 us (8%)
  local copies, waits for them, and re-layouts  3 us (2%)
    all_to_all x1, blocking collectives, lax.all_to_all(jnp.stack([local_block for _ in range(lax.axis_size('row')...  98.3 us
    psum x1, blocking collectives, shards(): lax.psum((weight_part, update_part), ('own', 'row'))  81.4 us
    reduce_or x1, other arithmetic, slot_select(): return jnp.any(joined, axis=0).astype(jnp.float32)  7.73 us
    reduce_sum x1, other arithmetic, shards(): update_sq = jnp.sum(direction * direction, axis=(2, 3))[0]  4.33 us

profile of v1, /device:TPU:1, one launch (start us, length us, event | category | flops | bytes accessed | tf_op | source)
XLA Modules:
  0.0 200.0 jit_solution(10478098668119659210)
XLA Ops:
  0.6 0.0 copy-start
  0.6 0.8 iota_compare_fusion.1
  1.4 0.7 fusion.4
  2.1 0.1 copy.14
  2.2 0.2 reduce_window_sum.11
  2.4 0.8 select_reduce_fusion
  3.3 7.7 %and_reduce_fusion = pred[32,8,14]{1,2,0:T(8,128)(4,1)S(1)} fusion(pred[127,14]{0,1:T(8,128)(4,1)S(1)} %iota_compare_fusion.1, pred[127,32,8]{0,2,1:T(8,128)(4,1)S(1)} %broadcast_and_fusion), kind=kLoop, calls=%fused_computation | loop fusion | flops 906752 | bytes 37874 | tf_op jit(solution)/shard_map/reduce_or | solution.py:41
  11.1 0.1 copy.15
  11.2 4.3 %multiply_reduce_fusion = (f32[8]{0:T(128)S(1)}, f32[1,8,16,2048]{3,2,1,0:T(8,128)S(1)}, f32[1,8,16,2048]{3,2,1,0:T(8,128)}, f32[1,8,16,2048]{3,2,1,0:T(8,128)}, f32[8]{0:T(128)S(1)}) fusion(f32[1,8,16,2048]{3,2,1,0:T(8,128)} %param.6, f32[1,8,16,2048]{3,2,1,0:T(8,128)} %param.8, bf16[1,8,16,2048]{3,2,1,0:T(8,128)(2,1)} %param.9, ...), kind=kLoop, calls=%fused_computation.5 | loop fusion | flops 4456432 | bytes 6815840 | tf_op jit(solution)/shard_map/reduce_sum | solution.py:54
  15.5 0.1 fusion.6
  15.6 81.4 %all-reduce = (f32[14]{0:T(128)S(1)}, f32[14]{0:T(128)S(1)}) all-reduce(f32[14]{0:T(128)S(1)} %get-tuple-element.8, f32[14]{0:T(128)S(1)} %get-tuple-element.7), channel_id=1, replica_groups=mesh['own'=32,'row'=8] {'own','row'}, use_global_device_ids=true, to_apply=%region_6.7 | all-reduce | flops 28 | bytes 224 | tf_op jit(solution)/shard_map/psum | solution.py:57
  97.0 0.5 add_divide_fusion
  97.5 0.0 copy-start.1
  97.5 0.1 fusion.7
  97.6 0.0 copy-done
  97.6 1.2 convert_bitcast_fusion
  98.9 0.5 stack.2
  99.4 0.0 copy-done.1
  99.4 98.3 %all_to_all.5 = bf16[8,1,8,16,2048]{4,3,2,1,0:T(8,128)(2,1)S(1)} all-to-all(bf16[8,1,8,16,2048]{4,3,2,1,0:T(8,128)(2,1)S(1)} %stack.2), channel_id=1, replica_groups=mesh['own'=32,'row'=8] {'row'}, dimensions={0} | all-to-all | bytes 8388608 | tf_op jit(solution)/shard_map/all_to_all | solution.py:18
  197.7 2.3 %copy.16 = bf16[8,1,8,16,2048]{4,3,0,2,1:T(8,128)(2,1)} copy(bf16[8,1,8,16,2048]{4,3,2,1,0:T(8,128)(2,1)S(1)} %all_to_all.5) | data formatting | bytes 8388608 | tf_op jit(solution)/shard_map/all_to_all | solution.py:18
  (5 shorter events, 0.1 us)
Async XLA Ops:
  0.6 97.0 %copy-start = (f32[1,8,16,2048]{3,2,1,0:T(8,128)S(1)}, f32[1,8,16,2048]{3,2,1,0:T(8,128)}, u32[]{:S(2)}) copy-start(f32[1,8,16,2048]{3,2,1,0:T(8,128)} %param.6) | copy-start | bytes 3145732
  97.5 1.9 copy-start.1
